TPU v7x, 32 devices: a whole 2x2x4 slice. The times are simulated.
32 devices in a mesh: fibre: 4 (over z), cols: 8 (over y, x, core).
Axes of the slice: x: 2, y: 2, z: 4, core: 2. Of those that a mesh axis runs over, the one named last changes fastest.
Arguments:
- tensor: float32 [512, 8, 4, 2048], P('fibre', 'cols'), may hold values from -6 to 6
- initial: float32 [512, 64], replicated, may hold values from -6 to 6
Outputs:
- core_slab: float32 [64, 8, 4, 2048], P(None, 'cols', 'fibre')
- basis: float32 [512, 64], replicated
All inputs are finite; a program needn't handle non-finite values.
Results may differ from a plain program's by a relative error of at most 0.0002.
Values sent between devices are 32-bit elements; how exact they have to be, the bound alone decides.
No kernel may reach another device: no remote copies, remote signals or barrier semaphores. Data moves between devices by JAX's collectives and lax.ppermute only.
A program may use at most 64 MiB of HBM per device.

v0:
```python
import jax
import jax.numpy as jnp
from jax import lax
from jax.sharding import PartitionSpec as P

ITERS = 2


def orthonormal(product):
    squares = jnp.dot(product.T, product, precision=lax.Precision.HIGHEST)
    lower = jnp.linalg.cholesky(squares)
    return lax.linalg.triangular_solve(
        lower, product, left_side=False, lower=True, transpose_a=True
    )


def shards(tensor, initial):
    highest = lax.Precision.HIGHEST
    gathered = lax.all_to_all(tensor, "fibre", split_axis=2, concat_axis=0, tiled=True)
    modes = gathered.shape[0]
    width = gathered.shape[3]
    columns = gathered.reshape(modes, width)
    local_gram = jnp.dot(columns, columns.T, precision=highest)
    gram = lax.psum(local_gram, ("fibre", "cols"))
    basis = initial
    for step in range(ITERS):
        basis = orthonormal(jnp.dot(gram, basis, precision=highest))
    ranks = basis.shape[1]
    core_slab = jnp.dot(basis.T, columns, precision=highest).reshape(ranks, 1, 1, width)
    return (core_slab, basis)


def solution(mesh):
    placed = (P("fibre", "cols", None, None), P())
    return jax.shard_map(
        shards,
        mesh=mesh,
        in_specs=placed,
        out_specs=(P(None, "cols", "fibre", None), P()),
        check_vma=False,
    )
```

profile of v0, /device:TPU:0, one launch (start us, length us, event | category | flops | bytes accessed | tf_op | source)
XLA Modules:
  0.0 294.8 jit_solution(3393844328094002086)
XLA Ops:
  7.2 0.0 copy-start
  7.2 0.0 all-reduce.2.cloned.1.call-start
  7.2 4.6 %copy.11 = f32[128,1,4,2048]{3,0,1,2:T(8,128)S(1)} copy(f32[128,1,4,2048]{3,2,1,0:T(4,128)} %param.5) | data formatting | bytes 8388608 | tf_op args[0]
  11.9 99.3 %all_to_all.15 = f32[128,1,4,2048]{3,0,1,2:T(8,128)S(1)} all-to-all(f32[128,1,4,2048]{3,0,1,2:T(8,128)S(1)} %copy.11), channel_id=1, replica_groups=mesh['fibre'=4,'cols'=8] {'fibre'}, dimensions={2} | all-to-all | bytes 8388608 | tf_op jit(solution)/shard_map/all_to_all | solution.py:19
  111.2 0.0 copy-start.1
  111.2 1.9 copy-done.1
  113.1 7.9 %fusion.8 = f32[512,512]{1,0:T(8,128)} fusion(f32[512,2048]{1,0:T(8,128)S(1)} %bitcast.43), kind=kOutput, calls=%fused_computation.20 | convolution fusion | flops 6442450944 | bytes 5242880 | tf_op jit(solution)/shard_map/dot_general | solution.py:23
  121.0 0.0 all-reduce.2.cloned.1.call-update
  121.0 130.2 %all-reduce.2.cloned.1.call-done = f32[512,512]{1,0:T(8,128)} async-done(((f32[512,512]{1,0:T(8,128)}), f32[512,512]{1,0:T(8,128)}) %all-reduce.2.cloned.1.call-update) | async-done | bytes 1048592 | tf_op jit(solution)/shard_map/psum | solution.py:24
  251.3 0.0 copy-done
  251.3 2.4 fusion.9
  253.6 0.3 fusion.10
  253.9 0.1 copy.12
  254.0 5.8 %cholesky.44 = f32[64,64]{1,0:T(8,128)S(1)} custom-call(f32[64,64]{1,0:T(8,128)S(1)} %fusion.5), custom_call_target="Cholesky" | custom-call | tf_op jit(solution)/shard_map/jit(cholesky)/cholesky | solution.py:11
  259.9 0.6 compare_reduce_fusion.1
  260.5 0.7 fusion
  261.2 4.9 %custom-call.6 = f32[1,64,64]{1,2,0:T(8,128)S(1)} custom-call(f32[1,64,64]{2,1,0:T(8,128)S(1)} %fusion), custom_call_target="InvertDiagBlocksLowerTriangular" | custom-call | tf_op jit(solution)/shard_map/triangular_solve/custom-call.0 | solution.py:12
  266.1 0.3 convolution_bitcast_fusion.2
  266.4 2.4 fusion.11
  268.8 0.3 fusion.12
  269.0 0.1 copy.13
  269.1 6.0 %cholesky.55 = f32[64,64]{1,0:T(8,128)S(1)} custom-call(f32[64,64]{1,0:T(8,128)S(1)} %fusion.3), custom_call_target="Cholesky" | custom-call | tf_op jit(solution)/shard_map/jit(cholesky)/cholesky | solution.py:11
  275.2 0.6 compare_reduce_fusion
  275.8 0.7 fusion.1
  276.5 4.9 %custom-call.7 = f32[1,64,64]{1,2,0:T(8,128)S(1)} custom-call(f32[1,64,64]{2,1,0:T(8,128)S(1)} %fusion.1), custom_call_target="InvertDiagBlocksLowerTriangular" | custom-call | tf_op jit(solution)/shard_map/triangular_solve/custom-call.0 | solution.py:12
  281.4 0.3 convolution_bitcast_fusion.1
  281.7 0.0 copy-start.2
  281.8 4.9 %convolution_bitcast_fusion = f32[64,1,1,2048]{3,0,2,1:T(8,128)S(1)} fusion(f32[512,64]{0,1:T(8,128)S(1)} %convolution_bitcast_fusion.1, f32[512,2048]{1,0:T(8,128)} %bitcast.44), kind=kOutput, calls=%fused_computation | convolution fusion | flops 805306368 | bytes 4849664 | tf_op jit(solution)/shard_map/dot_general | solution.py:29
  286.6 1.3 copy.14
  288.0 0.0 copy-done.2
  (4 shorter events, 0.1 us)
Async XLA Ops:
  7.2 244.1 %copy-start = (f32[512,64]{0,1:T(8,128)S(1)}, f32[512,64]{0,1:T(8,128)}, u32[]{:S(2)}) copy-start(f32[512,64]{0,1:T(8,128)} %param.6) | copy-start | bytes 393220
  7.2 244.1 %all-reduce.2.cloned.1.call-start = ((), (), s32[]{:S(2)}) async-start(), calls=%async_computation.1 | async-start | bytes 2097152 | tf_op jit(solution)/shard_map/psum | solution.py:24
  111.2 1.9 copy-start.1
  281.7 6.2 %copy-start.2 = (f32[512,64]{0,1:T(8,128)}, f32[512,64]{0,1:T(8,128)S(1)}, u32[]{:S(2)}) copy-start(f32[512,64]{0,1:T(8,128)S(1)} %convolution_bitcast_fusion.1) | copy-start | bytes 393220
Sparse Core Ops, SparseCore 0:
  121.2 130.0 all-reduce.1
where the time goes:
time: 295 us
  waiting for transfers between devices  130 us (44%)
  blocking collectives  99.3 us (34%)
  other arithmetic  24.4 us (8%)
  matrix products  18.7 us (6%)
  between operations  14.1 us (5%)
  local copies, waits for them, and re-layouts  8.07 us (3%)
    psum x1, waiting for transfers between devices, shards(): gram = lax.psum(local_gram, ('fibre', 'cols'))  130 us
    all_to_all x1, blocking collectives, shards(): lax.all_to_all(tensor, 'fibre', split_axis=2, concat_axis=0, tiled=True)  99.3 us
    another operation x6, other arithmetic, orthonormal(): lower = jnp.linalg.cholesky(squares)  13.2 us
    another operation x4, other arithmetic, orthonormal(): lax.linalg.triangular_solve(lower, product, left_side=False, lower=True,...  11.1 us
    dot_general x1, matrix products, shards(): local_gram = jnp.dot(columns, columns.T, precision=highest)  7.93 us
    unnamed x8, local copies, waits for them, and re-layouts  7.92 us
  transfers between devices with their start and end apart: 1, of which 1 were waited for; matrix products, arithmetic and copies ran while one was open for 0% of the time, Pallas kernels for 0%

commit v1 on v0

--- a/solution.py
+++ b/solution.py
@@ -21,7 +21,8 @@
     width = gathered.shape[3]
     columns = gathered.reshape(modes, width)
     local_gram = jnp.dot(columns, columns.T, precision=highest)
-    gram = lax.psum(local_gram, ("fibre", "cols"))
+    inner = lax.psum(local_gram, "cols")
+    gram = lax.psum(inner, "fibre")
     basis = initial
     for step in range(ITERS):
         basis = orthonormal(jnp.dot(gram, basis, precision=highest))

time: 295 us -> 274 us (0.929)
  waiting for transfers between devices: 130 us -> 110 us
    psum x1 -> x2, waiting for transfers between devices: 130 us -> 109 us  [the longest x1 56 us: shards(): inner = lax.psum(local_gram, 'cols')]
  transfers between devices with their start and end apart: 1 -> 2, of which waited for: 1 -> 2; matrix products, arithmetic and copies ran while one was open for 0% -> 0% of each run, Pallas kernels for 0% -> 0%
where the time goes in v1:
time: 274 us
  waiting for transfers between devices  110 us (40%)
  blocking collectives  99.3 us (36%)
  other arithmetic  24.2 us (9%)
  matrix products  18.7 us (7%)
  between operations  14.1 us (5%)
  local copies, waits for them, and re-layouts  8.07 us (3%)
    all_to_all x1, blocking collectives, shards(): lax.all_to_all(tensor, 'fibre', split_axis=2, concat_axis=0, tiled=True)  99.3 us
    psum x1, waiting for transfers between devices, shards(): inner = lax.psum(local_gram, 'cols')  56 us
    psum x1, waiting for transfers between devices, shards(): gram = lax.psum(inner, 'fibre')  53.5 us
    another operation x6, other arithmetic, orthonormal(): lower = jnp.linalg.cholesky(squares)  13 us
    another operation x4, other arithmetic, orthonormal(): lax.linalg.triangular_solve(lower, product, left_side=False, lower=True,...  11.1 us
    dot_general x1, matrix products, shards(): local_gram = jnp.dot(columns, columns.T, precision=highest)  7.93 us
    unnamed x8, local copies, waits for them, and re-layouts  7.92 us
  transfers between devices with their start and end apart: 2, of which 2 were waited for; matrix products, arithmetic and copies ran while one was open for 0% of the time, Pallas kernels for 0%

profile of v1, /device:TPU:0, one launch (start us, length us, event | category | flops | bytes accessed | tf_op | source)
XLA Modules:
  0.0 274.1 jit_solution(10527738758736755894)
XLA Ops:
  7.2 0.0 copy-start
  7.2 0.0 all-reduce.3.cloned.1.call-start
  7.2 4.6 %copy.11 = f32[128,1,4,2048]{3,0,1,2:T(8,128)S(1)} copy(f32[128,1,4,2048]{3,2,1,0:T(4,128)} %param.5) | data formatting | bytes 8388608 | tf_op args[0]
  11.9 99.3 %all_to_all.15 = f32[128,1,4,2048]{3,0,1,2:T(8,128)S(1)} all-to-all(f32[128,1,4,2048]{3,0,1,2:T(8,128)S(1)} %copy.11), channel_id=1, replica_groups=mesh['fibre'=4,'cols'=8] {'fibre'}, dimensions={2} | all-to-all | bytes 8388608 | tf_op jit(solution)/shard_map/all_to_all | solution.py:19
  111.2 0.0 copy-start.1
  111.2 1.9 copy-done.1
  113.1 7.9 %fusion.8 = f32[512,512]{1,0:T(8,128)} fusion(f32[512,2048]{1,0:T(8,128)S(1)} %bitcast.43), kind=kOutput, calls=%fused_computation.20 | convolution fusion | flops 6442450944 | bytes 5242880 | tf_op jit(solution)/shard_map/dot_general | solution.py:23
  121.0 0.0 all-reduce.3.cloned.1.call-update
  121.0 0.2 all-reduce.5.cloned.1.call-start
  121.3 56.0 %all-reduce.3.cloned.1.call-done = f32[512,512]{1,0:T(8,128)} async-done(((f32[512,512]{1,0:T(8,128)}), f32[512,512]{1,0:T(8,128)}) %all-reduce.3.cloned.1.call-update) | async-done | bytes 1048592 | tf_op jit(solution)/shard_map/psum | solution.py:24
  177.3 0.0 all-reduce.5.cloned.1.call-update
  177.3 53.5 %all-reduce.5.cloned.1.call-done = f32[512,512]{1,0:T(8,128)} async-done(((f32[512,512]{1,0:T(8,128)}), f32[512,512]{1,0:T(8,128)}) %all-reduce.5.cloned.1.call-update) | async-done | bytes 1048592 | tf_op jit(solution)/shard_map/psum | solution.py:25
  230.8 0.0 copy-done
  230.8 2.4 fusion.9
  233.1 0.3 fusion.10
  233.4 0.1 copy.12
  233.5 5.8 %cholesky.44 = f32[64,64]{1,0:T(8,128)S(1)} custom-call(f32[64,64]{1,0:T(8,128)S(1)} %fusion.5), custom_call_target="Cholesky" | custom-call | tf_op jit(solution)/shard_map/jit(cholesky)/cholesky | solution.py:11
  239.4 0.6 compare_reduce_fusion.1
  240.0 0.7 fusion
  240.7 4.9 %custom-call.6 = f32[1,64,64]{1,2,0:T(8,128)S(1)} custom-call(f32[1,64,64]{2,1,0:T(8,128)S(1)} %fusion), custom_call_target="InvertDiagBlocksLowerTriangular" | custom-call | tf_op jit(solution)/shard_map/triangular_solve/custom-call.0 | solution.py:12
  245.6 0.3 convolution_bitcast_fusion.2
  245.9 2.4 fusion.11
  248.3 0.3 fusion.12
  248.5 0.1 copy.13
  248.6 5.8 %cholesky.55 = f32[64,64]{1,0:T(8,128)S(1)} custom-call(f32[64,64]{1,0:T(8,128)S(1)} %fusion.3), custom_call_target="Cholesky" | custom-call | tf_op jit(solution)/shard_map/jit(cholesky)/cholesky | solution.py:11
  254.5 0.6 compare_reduce_fusion
  255.2 0.7 fusion.1
  255.8 4.9 %custom-call.7 = f32[1,64,64]{1,2,0:T(8,128)S(1)} custom-call(f32[1,64,64]{2,1,0:T(8,128)S(1)} %fusion.1), custom_call_target="InvertDiagBlocksLowerTriangular" | custom-call | tf_op jit(solution)/shard_map/triangular_solve/custom-call.0 | solution.py:12
  260.7 0.3 convolution_bitcast_fusion.1
  261.1 0.0 copy-start.2
  261.1 4.9 %convolution_bitcast_fusion = f32[64,1,1,2048]{3,0,2,1:T(8,128)S(1)} fusion(f32[512,64]{0,1:T(8,128)S(1)} %convolution_bitcast_fusion.1, f32[512,2048]{1,0:T(8,128)} %bitcast.44), kind=kOutput, calls=%fused_computation | convolution fusion | flops 805306368 | bytes 4849664 | tf_op jit(solution)/shard_map/dot_general | solution.py:30
  265.9 1.3 copy.14
  267.3 0.0 copy-done.2
  (4 shorter events, 0.1 us)
Async XLA Ops:
  7.2 223.6 %copy-start = (f32[512,64]{0,1:T(8,128)S(1)}, f32[512,64]{0,1:T(8,128)}, u32[]{:S(2)}) copy-start(f32[512,64]{0,1:T(8,128)} %param.6) | copy-start | bytes 393220
  7.2 170.1 %all-reduce.3.cloned.1.call-start = ((), (), s32[]{:S(2)}) async-start(), calls=%async_computation.1 | async-start | bytes 2097152 | tf_op jit(solution)/shard_map/psum | solution.py:24
  111.2 1.9 copy-start.1
  121.0 109.7 %all-reduce.5.cloned.1.call-start = ((), (), s32[]{:S(2)}) async-start(), calls=%async_computation.2 | async-start | bytes 2097152 | tf_op jit(solution)/shard_map/psum | solution.py:25
  261.1 6.2 %copy-start.2 = (f32[512,64]{0,1:T(8,128)}, f32[512,64]{0,1:T(8,128)S(1)}, u32[]{:S(2)}) copy-start(f32[512,64]{0,1:T(8,128)S(1)} %convolution_bitcast_fusion.1) | copy-start | bytes 393220
Sparse Core Ops, SparseCore 0:
  121.2 56.0 all-reduce.2
  179.6 51.1 all-reduce.4
